TPU v7x, 128 devices: a whole 4x4x4 slice. The times are simulated.
128 devices in a mesh: layer: 4 (over x_hi, core), feat: 16 (over z, y), par: 2 (over x_lo).
Axes of the slice: x: 4 (x_hi: 2, x_lo: 2; x = x_hi * 2 + x_lo), y: 4, z: 4, core: 2. Of those that a mesh axis runs over, the one named last changes fastest.
Arguments:
- residual: bfloat16 [4, 512, 2304], P('layer'), may hold values from -6 to 6
- norm_gain: float32 [4, 2304], P('layer'), may hold values from 0.5 to 1.5
- gate_weight: bfloat16 [4, 2304, 9216], P('layer', None, ('feat', 'par')), may hold values from -0.125 to 0.125
- up_weight: bfloat16 [4, 2304, 9216], P('layer', None, ('feat', 'par')), may hold values from -0.125 to 0.125
- down_weight: bfloat16 [4, 9216, 2304], P('layer', ('feat', 'par')), may hold values from -0.0625 to 0.0625
- enc_weight: float32 [4, 2304, 8192], P('layer', 'par', 'feat'), may hold values from -0.125 to 0.125
- enc_bias: float32 [4, 8192], P('layer', 'feat'), may hold values from -1 to 0.5
- dec_weight: bfloat16 [4, 2, 2, 8192, 2304], P('layer', 'par', None, 'feat'), may hold values from -0.0625 to 0.0625
- dec_bias: float32 [4, 2304], replicated, may hold values from -3 to 3
Outputs:
- enc_grad: float32 [4, 2304, 8192], P('layer', 'par', 'feat')
- enc_bias_grad: float32 [4, 8192], P('layer', 'feat')
- dec_grad: bfloat16 [4, 2, 2, 8192, 2304], P('layer', 'par', None, 'feat')
All inputs are finite; a program needn't handle non-finite values.
Results may differ from a plain program's by a relative error of at most 0.007.
Values may be sent and summed in bfloat16 or wider, within the bound.
A program may use at most 192 MiB of HBM per device.

v0:
```python
import jax
import jax.numpy as jnp
from jax import lax
from jax.sharding import PartitionSpec as P


def rms_normed(rows_in, gain_row):
    values = rows_in.astype(jnp.float32)
    scaling = lax.rsqrt(jnp.mean(values * values, axis=-1, keepdims=True) + 1e-06)
    return (values * scaling * gain_row).astype(jnp.bfloat16)


def shards(
    residual,
    norm_gain,
    gate_weight,
    up_weight,
    down_weight,
    enc_weight,
    enc_bias,
    dec_weight,
    dec_bias,
):
    highest = lax.Precision.HIGHEST
    source = lax.axis_index("layer")
    parity = lax.axis_index("par")
    slot_count = dec_weight.shape[2]
    normed = rms_normed(residual[0], norm_gain[0])
    tokens, model_width = normed.shape
    gate_value = jnp.dot(normed, gate_weight[0], preferred_element_type=jnp.float32)
    up_value = jnp.dot(normed, up_weight[0], preferred_element_type=jnp.float32)
    hidden = (jax.nn.gelu(gate_value, approximate=True) * up_value).astype(jnp.bfloat16)
    target_part = jnp.dot(hidden, down_weight[0], preferred_element_type=jnp.float32)
    half_width = enc_weight.shape[1]
    my_rows = lax.dynamic_slice_in_dim(normed, parity * half_width, half_width, 1).astype(
        jnp.float32
    )
    pre_part = jnp.dot(my_rows, enc_weight[0], precision=highest)
    pre_act = lax.psum(pre_part, "par") + enc_bias[0]
    positive = jnp.maximum(pre_act, 0.0)
    actives = (positive * positive).astype(jnp.bfloat16)
    slot_ids = jnp.arange(slot_count, dtype=jnp.int32)
    slot_live = 2 * slot_ids + parity >= source
    live_float = slot_live.astype(jnp.float32)
    decoders = dec_weight[0, 0]
    recon_parts = (
        jnp.einsum("tf,jfd->jtd", actives, decoders, preferred_element_type=jnp.float32)
        * live_float[:, None, None]
    )
    bias_slots = lax.dynamic_index_in_dim(
        dec_bias.reshape(slot_count, 2, model_width), parity, 1, keepdims=False
    )
    full_target = lax.psum(target_part, ("feat", "par"))
    all_targets = lax.all_gather(full_target[None], "layer", axis=0, tiled=True)
    target_slots = lax.dynamic_index_in_dim(
        all_targets.reshape(slot_count, 2, tokens, model_width), parity, 1, keepdims=False
    )
    summed_rows = lax.psum(recon_parts, ("layer", "feat"))
    err_full = summed_rows + bias_slots[:, None, :]
    err_full = err_full - target_slots
    errors = (err_full * 0.0625).astype(jnp.bfloat16)
    masked = errors * slot_live.astype(jnp.bfloat16)[:, None, None]
    back_part = jnp.einsum("jtd,jfd->tf", masked, decoders, preferred_element_type=jnp.float32)
    back_grad = lax.psum(back_part.astype(jnp.bfloat16), "par").astype(jnp.float32)
    d_pre = back_grad * 2.0 * positive
    enc_grad = lax.dot_general(my_rows, d_pre, (((0,), (0,)), ((), ())), precision=highest)
    bias_grad = jnp.sum(d_pre, axis=0)
    dec_grad = jnp.einsum(
        "tf,jtd->jfd", actives, masked, preferred_element_type=jnp.float32
    ).astype(jnp.bfloat16)
    return (enc_grad[None], bias_grad[None], dec_grad[None, None])


def solution(mesh):
    return jax.shard_map(
        shards,
        mesh=mesh,
        in_specs=(
            P("layer", None, None),
            P("layer", None),
            P("layer", None, ("feat", "par")),
            P("layer", None, ("feat", "par")),
            P("layer", ("feat", "par"), None),
            P("layer", "par", "feat"),
            P("layer", "feat"),
            P("layer", "par", None, "feat", None),
            P(),
        ),
        out_specs=(
            P("layer", "par", "feat"),
            P("layer", "feat"),
            P("layer", "par", None, "feat", None),
        ),
        check_vma=False,
    )
```

profile of v0, /device:TPU:1, one launch (start us, length us, event | category | flops | bytes accessed | tf_op | source)
XLA Modules:
  0.0 1276.6 jit_solution(10719600831375024537)
XLA Ops:
  7.2 0.0 copy-start
  7.2 0.0 all-reduce.5.cloned.1.call-start
  7.2 0.0 copy-start.6
  7.2 2.4 multiply_reduce_fusion
  9.6 4.2 convert_bitcast_fusion
  13.8 0.0 copy-done.6
  13.8 0.1 dynamic-slice
  13.9 0.0 copy-done
  13.9 4.9 fusion.12
  18.8 0.0 all-reduce.5.cloned.1.call-update
  18.9 0.0 copy-start.2
  18.9 0.0 all-reduce.9.cloned.1.call-start
  18.9 3.2 fusion.43
  22.2 0.0 copy-done.2
  22.2 6.3 convolution_bitcast_fusion
  28.4 0.0 copy-start.5
  28.4 0.0 all-reduce.9.cloned.1.call-update
  28.5 0.0 all-reduce.7.cloned.1.call-start
  28.5 40.3 %all-reduce.5.cloned.1.call-done = f32[512,512]{1,0:T(8,128)} async-done(((f32[512,512]{1,0:T(8,128)}), f32[512,512]{1,0:T(8,128)}) %all-reduce.5.cloned.1.call-update) | async-done | bytes 1048592 | tf_op jit(solution)/shard_map/psum | solution.py:39
  68.8 0.0 copy-done.5
  68.8 8.9 multiply_bitcast_fusion
  77.8 0.0 all-reduce.7.cloned.1.call-update
  77.8 0.0 copy-start.4
  77.8 0.0 all-gather.2.cloned.1.call-start
  77.8 314.6 %all-reduce.9.cloned.1.call-done = f32[1,512,2304]{2,1,0:T(8,128)} async-done(((f32[1,512,2304]{2,1,0:T(8,128)}), f32[1,512,2304]{2,1,0:T(8,128)}) %all-reduce.9.cloned.1.call-update) | async-done | bytes 4718608 | tf_op jit(solution)/shard_map/psum | solution.py:53
  392.4 0.0 all-gather.2.cloned.1.call-update
  392.5 0.2 all-reduce.11.cloned.1.call-start
  392.7 0.0 copy-done.4
  392.8 668.2 %all-reduce.7.cloned.1.call-done = f32[2,512,2304]{2,1,0:T(8,128)} async-done(((f32[2,512,2304]{2,1,0:T(8,128)}), f32[2,512,2304]{2,1,0:T(8,128)}) %all-reduce.7.cloned.1.call-update) | async-done | bytes 9437200 | tf_op jit(solution)/shard_map/psum | solution.py:58
  1061.0 149.9 %all-gather.2.cloned.1.call-done = f32[4,512,2304]{2,1,0:T(8,128)} async-done(((f32[1,512,2304]{2,1,0:T(8,128)}), f32[4,512,2304]{2,1,0:T(8,128)}) %all-gather.2.cloned.1.call-update) | async-done | bytes 18874384 | tf_op jit(solution)/shard_map/all_gather | solution.py:54
  1210.8 10.1 fusion.5
  1220.9 0.0 copy-start.3
  1220.9 7.3 fusion.22
  1228.2 0.0 all-reduce.11.cloned.1.call-update
  1228.2 0.0 copy-done.3
  1228.2 6.7 fusion.2
  1234.9 0.0 copy-start.1
  1234.9 6.8 copy.17
  1241.7 21.0 %all-reduce.11.cloned.1.call-done = bf16[512,512]{1,0:T(8,128)(2,1)} async-done(((bf16[512,512]{1,0:T(8,128)(2,1)}), bf16[512,512]{1,0:T(8,128)(2,1)}) %all-reduce.11.cloned.1.call-update) | async-done | bytes 524304 | tf_op jit(solution)/shard_map/psum | solution.py:64
  1262.7 1.8 fusion.48
  1264.6 5.5 convolution_bitcast_fusion.1
  1270.1 0.0 copy-done.1
  (7 shorter events, 0.1 us)
Async XLA Ops:
  7.2 6.7 copy-start
  7.2 61.7 %all-reduce.5.cloned.1.call-start = ((), (), s32[]{:S(2)}) async-start(), calls=%async_computation | async-start | bytes 2097152 | tf_op jit(solution)/shard_map/psum | solution.py:39
  7.2 6.5 copy-start.6
  18.9 3.3 copy-start.2
  18.9 373.6 %all-reduce.9.cloned.1.call-start = ((), (), s32[]{:S(2)}) async-start(), calls=%async_computation.2 | async-start | bytes 9437184 | tf_op jit(solution)/shard_map/psum | solution.py:53
  28.4 40.4 %copy-start.5 = (f32[1,512]{1,0:T(1,128)S(1)}, f32[1,512]{1,0:T(1,128)}, u32[]{:S(2)}) copy-start(f32[1,512]{1,0:T(1,128)} %param.15) | copy-start | bytes 6148
  28.5 1032.5 %all-reduce.7.cloned.1.call-start = ((), (), s32[]{:S(2)}) async-start(), calls=%async_computation.1 | async-start | bytes 18874368 | tf_op jit(solution)/shard_map/psum | solution.py:58
  77.8 314.9 %copy-start.4 = (f32[4,2304]{1,0:T(4,128)S(1)}, f32[4,2304]{1,0:T(4,128)}, u32[]{:S(2)}) copy-start(f32[4,2304]{1,0:T(4,128)} %param.17) | copy-start | bytes 110596
  77.8 1133.0 %all-gather.2.cloned.1.call-start = ((), (), s32[]{:S(2)}) async-start(), calls=%async_computation.3 | async-start | bytes 23592960 | tf_op jit(solution)/shard_map/all_gather | solution.py:54
  392.5 870.3 %all-reduce.11.cloned.1.call-start = ((), (), s32[]{:S(2)}) async-start(), calls=%async_computation.4 | async-start | bytes 1048576 | tf_op jit(solution)/shard_map/psum | solution.py:64
  1220.9 7.3 copy-start.3
  1234.9 35.2 %copy-start.1 = (f32[1,1152,512]{2,1,0:T(8,128)S(1)}, f32[1,1152,512]{2,1,0:T(8,128)}, u32[]{:S(2)}) copy-start(f32[1,1152,512]{2,1,0:T(8,128)} %param.14) | copy-start | bytes 7077892
Sparse Core Ops, SparseCore 0:
  19.0 49.8 all-reduce.4
  72.1 320.3 all-reduce.8
  395.1 665.8 all-reduce.6
  1062.6 148.1 all-gather.1
  1228.3 34.3 all-reduce.10
where the time goes:
time: 1280 us
  waiting for transfers between devices  1190 us (93%)
  matrix products  42.9 us (3%)
  other arithmetic  18.5 us (1%)
  between operations  13.9 us (1%)
    psum x1, waiting for transfers between devices, shards(): summed_rows = lax.psum(recon_parts, ('layer', 'feat'))  668 us
    psum x1, waiting for transfers between devices, shards(): full_target = lax.psum(target_part, ('feat', 'par'))  315 us
    all_gather x1, waiting for transfers between devices, shards(): all_targets = lax.all_gather(full_target[None], 'layer', axis=0, tiled=True)  150 us
    psum x1, waiting for transfers between devices, shards(): pre_act = lax.psum(pre_part, 'par') + enc_bias[0]  40.3 us
  transfers between devices with their start and end apart: 5, of which 5 were waited for; matrix products, arithmetic and copies ran while one was open for 3% of the time, Pallas kernels for 0%

commit v1 on v0

--- a/solution.py
+++ b/solution.py
@@ -50,7 +50,7 @@
     bias_slots = lax.dynamic_index_in_dim(
         dec_bias.reshape(slot_count, 2, model_width), parity, 1, keepdims=False
     )
-    full_target = lax.psum(target_part, ("feat", "par"))
+    full_target = lax.all_gather(target_part, ("feat", "par")).sum(axis=0)
     all_targets = lax.all_gather(full_target[None], "layer", axis=0, tiled=True)
     target_slots = lax.dynamic_index_in_dim(
         all_targets.reshape(slot_count, 2, tokens, model_width), parity, 1, keepdims=False

time: 1280 us -> 3900 us (3.05)
  waiting for transfers between devices: 1190 us -> 3760 us
  other arithmetic: 18.5 us -> 65.3 us
    all_gather x0 -> x1, waiting for transfers between devices: none -> 3040 us  [shards(): full_target = lax.all_gather(target_part, ('feat', 'par')).sum(axis=0)]
    psum x1 -> x0, waiting for transfers between devices: 315 us -> none  [shards(): full_target = lax.psum(target_part, ('feat', 'par'))]
    all_gather x1, waiting for transfers between devices: 150 us -> 0.01 us  [shards(): all_targets = lax.all_gather(full_target[None], 'layer', axis=0, tiled=True)]
    psum x1, waiting for transfers between devices: 668 us -> 542 us  [shards(): summed_rows = lax.psum(recon_parts, ('layer', 'feat'))]
    psum x1, waiting for transfers between devices: 40.3 us -> 141 us  [shards(): pre_act = lax.psum(pre_part, 'par') + enc_bias[0]]
    reduce_sum x0 -> x1, other arithmetic: none -> 47.9 us  [shards(): full_target = lax.all_gather(target_part, ('feat', 'par')).sum(axis=0)]
  transfers between devices with their start and end apart: 5 -> 5, of which waited for: 5 -> 4; matrix products, arithmetic and copies ran while one was open for 3% -> 2% of each run, Pallas kernels for 0% -> 0%
where the time goes in v1:
time: 3900 us
  waiting for transfers between devices  3760 us (96%)
  other arithmetic  65.3 us (2%)
  matrix products  43 us (1%)
    all_gather x1, waiting for transfers between devices, shards(): full_target = lax.all_gather(target_part, ('feat', 'par')).sum(axis=0)  3040 us
    psum x1, waiting for transfers between devices, shards(): summed_rows = lax.psum(recon_parts, ('layer', 'feat'))  542 us
    psum x1, waiting for transfers between devices, shards(): pre_act = lax.psum(pre_part, 'par') + enc_bias[0]  141 us
  transfers between devices with their start and end apart: 5, of which 4 were waited for; matrix products, arithmetic and copies ran while one was open for 2% of the time, Pallas kernels for 0%

profile of v1, /device:TPU:1, one launch (start us, length us, event | category | flops | bytes accessed | tf_op | source)
XLA Modules:
  0.0 3895.8 jit_solution(4474386518046987420)
XLA Ops:
  8.0 0.0 copy-start
  8.0 0.0 all-reduce.4.cloned.1.call-start
  8.1 0.0 copy-start.7
  8.1 2.4 multiply_reduce_fusion
  10.4 4.1 convert_bitcast_fusion
  14.6 0.0 copy-done.7
  14.6 0.1 dynamic-slice
  14.7 0.0 copy-done
  14.7 4.9 fusion.12
  19.6 0.0 all-reduce.4.cloned.1.call-update
  19.7 0.0 copy-start.2
  19.7 0.0 all-gather.5.cloned.1.call-start
  19.7 3.2 fusion.43
  23.0 0.0 copy-done.2
  23.0 6.3 fusion.17
  29.2 0.0 copy-start.6
  29.3 0.0 all-gather.5.cloned.1.call-update
  29.3 0.0 all-reduce.6.cloned.1.call-start
  29.3 140.6 %all-reduce.4.cloned.1.call-done = f32[512,512]{1,0:T(8,128)} async-done(((f32[512,512]{1,0:T(8,128)}), f32[512,512]{1,0:T(8,128)}) %all-reduce.4.cloned.1.call-update) | async-done | bytes 1048592 | tf_op jit(solution)/shard_map/psum | solution.py:39
  170.0 0.0 copy-done.6
  170.0 8.9 multiply_bitcast_fusion
  178.9 0.0 all-reduce.6.cloned.1.call-update
  178.9 0.0 all-gather.7.cloned.1.call-start
  179.0 3036.1 %all-gather.5.cloned.1.call-done = f32[16384,2304]{1,0:T(8,128)} async-done(((f32[512,2304]{1,0:T(8,128)}), f32[16384,2304]{1,0:T(8,128)}) %all-gather.5.cloned.1.call-update) | async-done | bytes 150994960 | tf_op jit(solution)/shard_map/all_gather | solution.py:53
  3215.1 47.9 %reduce_sum.28 = f32[512,2304]{1,0:T(8,128)} reduce(f32[32,512,2304]{2,1,0:T(8,128)} %bitcast.10, f32[]{:T(128)} %constant.16.clone.1), dimensions={0}, to_apply=%region_3.4 | reduce | flops 36569088 | bytes 155713536 | tf_op jit(solution)/shard_map/reduce_sum | solution.py:53
  3263.0 0.0 copy-start.5
  3263.0 0.0 all-gather.7.cloned.1.call-update
  3263.0 0.2 all-reduce.8.cloned.1.call-start
  3263.3 0.5 copy-done.5
  3263.9 542.1 %all-reduce.6.cloned.1.call-done = f32[2,512,2304]{2,1,0:T(8,128)} async-done(((f32[2,512,2304]{2,1,0:T(8,128)}), f32[2,512,2304]{2,1,0:T(8,128)}) %all-reduce.6.cloned.1.call-update) | async-done | bytes 9437200 | tf_op jit(solution)/shard_map/psum | solution.py:58
  3806.0 0.0 all-gather.7.cloned.1.call-done
  3806.0 10.1 fusion.5
  3816.1 0.0 copy-start.3
  3816.1 7.3 fusion.23
  3823.3 0.0 all-reduce.8.cloned.1.call-update
  3823.3 0.0 copy-done.3
  3823.4 6.8 fusion.2
  3830.1 0.0 copy-start.1
  3830.1 6.8 copy.15
  3836.9 45.4 %all-reduce.8.cloned.1.call-done = bf16[512,512]{1,0:T(8,128)(2,1)} async-done(((bf16[512,512]{1,0:T(8,128)(2,1)}), bf16[512,512]{1,0:T(8,128)(2,1)}) %all-reduce.8.cloned.1.call-update) | async-done | bytes 524304 | tf_op jit(solution)/shard_map/psum | solution.py:64
  3882.2 0.0 copy-start.4
  3882.2 5.6 convolution_bitcast_fusion
  3887.8 0.0 copy-done.4
  3887.8 0.8 fusion.48
  3888.6 0.0 copy-done.1
  (7 shorter events, 0.1 us)
Async XLA Ops:
  8.0 6.7 copy-start
  8.0 162.0 %all-reduce.4.cloned.1.call-start = ((), (), s32[]{:S(2)}) async-start(), calls=%async_computation | async-start | bytes 2097152 | tf_op jit(solution)/shard_map/psum | solution.py:39
  8.1 6.5 copy-start.7
  19.7 3.3 copy-start.2
  19.7 3195.4 %all-gather.5.cloned.1.call-start = ((), (), s32[]{:S(2)}) async-start(), calls=%async_computation.3 | async-start | bytes 155713536 | tf_op jit(solution)/shard_map/all_gather | solution.py:53
  29.2 140.7 %copy-start.6 = (f32[1,512]{1,0:T(1,128)S(1)}, f32[1,512]{1,0:T(1,128)}, u32[]{:S(2)}) copy-start(f32[1,512]{1,0:T(1,128)} %param.15) | copy-start | bytes 6148
  29.3 3776.7 %all-reduce.6.cloned.1.call-start = ((), (), s32[]{:S(2)}) async-start(), calls=%async_computation.1 | async-start | bytes 18874368 | tf_op jit(solution)/shard_map/psum | solution.py:58
  178.9 3627.1 %all-gather.7.cloned.1.call-start = ((), (), s32[]{:S(2)}) async-start(), calls=%async_computation.4 | async-start | bytes 23592960 | tf_op jit(solution)/shard_map/all_gather | solution.py:54
  3263.0 0.8 copy-start.5
  3263.0 619.2 %all-reduce.8.cloned.1.call-start = ((), (), s32[]{:S(2)}) async-start(), calls=%async_computation.2 | async-start | bytes 1048576 | tf_op jit(solution)/shard_map/psum | solution.py:64
  3816.1 7.3 copy-start.3
  3830.1 58.5 %copy-start.1 = (f32[1,1152,512]{2,1,0:T(8,128)S(1)}, f32[1,1152,512]{2,1,0:T(8,128)}, u32[]{:S(2)}) copy-start(f32[1,1152,512]{2,1,0:T(8,128)} %param.14) | copy-start | bytes 7077892
  3882.2 5.6 copy-start.4
Sparse Core Ops, SparseCore 0:
  19.8 150.1 all-reduce.3
  179.0 3626.8 all-reduce.5
  3823.5 58.7 all-reduce.7
Sparse Core Ops, SparseCore 1:
  29.4 3185.7 all-gather.4
  3263.1 134.2 all-gather.6

commit v2 on v0

--- a/solution.py
+++ b/solution.py
@@ -50,7 +50,8 @@
     bias_slots = lax.dynamic_index_in_dim(
         dec_bias.reshape(slot_count, 2, model_width), parity, 1, keepdims=False
     )
-    full_target = lax.psum(target_part, ("feat", "par"))
+    one_axis = lax.psum(target_part, "feat")
+    full_target = lax.psum(one_axis, "par")
     all_targets = lax.all_gather(full_target[None], "layer", axis=0, tiled=True)
     target_slots = lax.dynamic_index_in_dim(
         all_targets.reshape(slot_count, 2, tokens, model_width), parity, 1, keepdims=False

time: 1280 us -> 1160 us (0.906)
  waiting for transfers between devices: 1190 us -> 1070 us
    psum x2, waiting for transfers between devices: 355 us -> 256 us  [the longest x1 152 us: shards(): full_target = lax.psum(one_axis, 'par')]
    psum x1, waiting for transfers between devices: 668 us -> 646 us  [shards(): summed_rows = lax.psum(recon_parts, ('layer', 'feat'))]
  transfers between devices with their start and end apart: 5 -> 5, of which waited for: 5 -> 5; matrix products, arithmetic and copies ran while one was open for 3% -> 2% of each run, Pallas kernels for 0% -> 0%
where the time goes in v2:
time: 1160 us
  waiting for transfers between devices  1070 us (92%)
  matrix products  41.9 us (4%)
  other arithmetic  17 us (1%)
  between operations  13.9 us (1%)
    psum x1, waiting for transfers between devices, shards(): summed_rows = lax.psum(recon_parts, ('layer', 'feat'))  646 us
    psum x1, waiting for transfers between devices, shards(): full_target = lax.psum(one_axis, 'par')  152 us
    all_gather x1, waiting for transfers between devices, shards(): all_targets = lax.all_gather(full_target[None], 'layer', axis=0, tiled=True)  150 us
    psum x1, waiting for transfers between devices, shards(): one_axis = lax.psum(target_part, 'feat')  104 us
  transfers between devices with their start and end apart: 5, of which 5 were waited for; matrix products, arithmetic and copies ran while one was open for 2% of the time, Pallas kernels for 0%

profile of v2, /device:TPU:1, one launch (start us, length us, event | category | flops | bytes accessed | tf_op | source)
XLA Modules:
  0.0 1155.6 jit_solution(15705061451066129697)
XLA Ops:
  7.2 0.0 copy-start
  7.2 0.0 all-reduce.8.cloned.1.call-start
  7.2 2.4 multiply_reduce_fusion
  9.6 0.7 reduce
  10.3 3.1 fusion.43
  13.4 7.0 fusion.17
  20.4 0.0 all-reduce.8.cloned.1.call-update
  20.4 0.0 all-reduce.12.cloned.1.call-start
  20.5 0.1 dynamic-slice
  20.6 2.0 convert_bitcast_fusion
  22.6 0.0 copy-start.2
  22.6 2.1 copy-done.2
  24.7 0.0 copy-done
  24.7 0.0 copy-start.5
  24.7 3.3 fusion.12
  28.1 104.1 %all-reduce.8.cloned.1.call-done = f32[512,2304]{1,0:T(8,128)} async-done(((f32[512,2304]{1,0:T(8,128)}), f32[512,2304]{1,0:T(8,128)}) %all-reduce.8.cloned.1.call-update) | async-done | bytes 4718608 | tf_op jit(solution)/shard_map/psum | solution.py:53
  132.1 0.0 all-reduce.12.cloned.1.call-update
  132.1 0.0 all-reduce.6.cloned.1.call-start
  132.2 151.8 %all-reduce.12.cloned.1.call-done = (f32[1,512,2304]{2,1,0:T(8,128)}, f32[512,512]{1,0:T(8,128)}) async-done(((f32[1,512,2304]{2,1,0:T(8,128)}, f32[512,512]{1,0:T(8,128)}), (f32[1,512,2304]{2,1,0:T(8,128)}, f32[512,512]{1,0:T(8,128)})) %all-reduce.12.cloned.1.call-update) | async-done | bytes 5767184 | tf_op jit(solution)/shard_map/psum | solution.py:54
  284.0 0.0 copy-done.5
  284.0 8.9 multiply_bitcast_fusion
  293.0 0.0 all-reduce.6.cloned.1.call-update
  293.0 0.0 copy-start.4
  293.0 0.0 all-gather.2.cloned.1.call-start
  293.0 0.5 all-gather.2.cloned.1.call-update
  293.6 0.2 all-reduce.10.cloned.1.call-start
  293.8 0.0 copy-done.4
  293.9 646.4 %all-reduce.6.cloned.1.call-done = f32[2,512,2304]{2,1,0:T(8,128)} async-done(((f32[2,512,2304]{2,1,0:T(8,128)}), f32[2,512,2304]{2,1,0:T(8,128)}) %all-reduce.6.cloned.1.call-update) | async-done | bytes 9437200 | tf_op jit(solution)/shard_map/psum | solution.py:59
  940.3 149.5 %all-gather.2.cloned.1.call-done = f32[4,512,2304]{2,1,0:T(8,128)} async-done(((f32[1,512,2304]{2,1,0:T(8,128)}), f32[4,512,2304]{2,1,0:T(8,128)}) %all-gather.2.cloned.1.call-update) | async-done | bytes 18874384 | tf_op jit(solution)/shard_map/all_gather | solution.py:55
  1089.8 10.1 fusion.5
  1099.9 0.0 copy-start.3
  1099.9 7.3 fusion.23
  1107.2 0.0 all-reduce.10.cloned.1.call-update
  1107.2 0.0 copy-done.3
  1107.2 6.7 fusion.2
  1113.9 0.0 copy-start.1
  1113.9 6.8 copy.17
  1120.7 21.0 %all-reduce.10.cloned.1.call-done = bf16[512,512]{1,0:T(8,128)(2,1)} async-done(((bf16[512,512]{1,0:T(8,128)(2,1)}), bf16[512,512]{1,0:T(8,128)(2,1)}) %all-reduce.10.cloned.1.call-update) | async-done | bytes 524304 | tf_op jit(solution)/shard_map/psum | solution.py:65
  1141.7 1.8 fusion.48
  1143.6 5.5 convolution_bitcast_fusion
  1149.1 0.0 copy-done.1
  (6 shorter events, 0.1 us)
Async XLA Ops:
  7.2 17.6 %copy-start = (f32[1,1152,512]{2,1,0:T(8,128)S(1)}, f32[1,1152,512]{2,1,0:T(8,128)}, u32[]{:S(2)}) copy-start(f32[1,1152,512]{2,1,0:T(8,128)} %param.14) | copy-start | bytes 7077892
  7.2 124.9 %all-reduce.8.cloned.1.call-start = ((), (), s32[]{:S(2)}) async-start(), calls=%async_computation.1 | async-start | bytes 9437184 | tf_op jit(solution)/shard_map/psum | solution.py:53
  20.4 263.6 %all-reduce.12.cloned.1.call-start = ((), (), s32[]{:S(2)}) async-start(), calls=%async_computation.4 | async-start | bytes 11534336 | tf_op jit(solution)/shard_map/psum | solution.py:54
  22.6 2.2 copy-start.2
  24.7 259.3 %copy-start.5 = (f32[1,512]{1,0:T(1,128)S(1)}, f32[1,512]{1,0:T(1,128)}, u32[]{:S(2)}) copy-start(f32[1,512]{1,0:T(1,128)} %param.15) | copy-start | bytes 6148
  132.1 808.2 %all-reduce.6.cloned.1.call-start = ((), (), s32[]{:S(2)}) async-start(), calls=%async_computation | async-start | bytes 18874368 | tf_op jit(solution)/shard_map/psum | solution.py:59
  293.0 0.8 copy-start.4
  293.0 796.8 %all-gather.2.cloned.1.call-start = ((), (), s32[]{:S(2)}) async-start(), calls=%async_computation.2 | async-start | bytes 23592960 | tf_op jit(solution)/shard_map/all_gather | solution.py:55
  293.6 848.1 %all-reduce.10.cloned.1.call-start = ((), (), s32[]{:S(2)}) async-start(), calls=%async_computation.3 | async-start | bytes 1048576 | tf_op jit(solution)/shard_map/psum | solution.py:65
  1099.9 7.3 copy-start.3
  1113.9 35.2 %copy-start.1 = (f32[1,1152,512]{2,1,0:T(8,128)S(1)}, f32[1,1152,512]{2,1,0:T(8,128)}, u32[]{:S(2)}) copy-start(f32[1,1152,512]{2,1,0:T(8,128)} %param.14) | copy-start | bytes 7077892
Sparse Core Ops, SparseCore 0:
  20.6 111.5 all-reduce.7
  135.5 148.4 all-reduce.11
  293.1 647.1 all-reduce.5
  941.8 147.9 all-gather.1
  1107.3 34.3 all-reduce.9
